TPU v7x, 32 devices: a whole 2x2x4 slice. The times are simulated.
32 devices in a mesh: seq: 8 (over z, x), fsdp: 4 (over y, core).
Axes of the slice: x: 2, y: 2, z: 4, core: 2. Of those that a mesh axis runs over, the one named last changes fastest.
Arguments:
- inputs: bfloat16 [3, 2048, 8192], P(None, 'seq', 'fsdp'), may hold values from -6 to 6
- grad_out: bfloat16 [2048, 8192], P('seq', 'fsdp'), may hold values from -6 to 6
- filters: bfloat16 [128, 8192], P('fsdp'), may hold values from -0.5 to 0.5
- short_weights: bfloat16 [3, 3, 8192], P(None, None, 'fsdp'), may hold values from -3.5 to 3.5
Outputs:
- grad_inputs: bfloat16 [3, 2048, 8192], P(None, 'seq', 'fsdp')
- grad_filters: float32 [128, 8192], P('fsdp')
- grad_short: float32 [3, 3, 8192], P(None, None, 'fsdp')
All inputs are finite; a program needn't handle non-finite values.
Results may differ from a plain program's by a relative error of at most 0.0057.
Values may be sent and summed in bfloat16 or wider, within the bound.
No kernel may reach another device: no remote copies, remote signals or barrier semaphores. Data moves between devices by JAX's collectives and lax.ppermute only.
A program may use at most 64 MiB of HBM per device.

v0:
```python
import jax
import jax.numpy as jnp
from jax import lax
from jax.sharding import PartitionSpec as P

FILTER_LEN = 128
SHORT_LEN = 3


def from_behind(block, axis, distance):
    devices = range(lax.axis_size(axis))
    route = [(i - distance, i) for i in devices if i - distance in devices]
    return lax.ppermute(block, axis, route)


def depthwise(signal, kernel):
    result = lax.conv_general_dilated(
        signal[None],
        kernel[:, None, :],
        (1,),
        "VALID",
        dimension_numbers=("NWC", "WIO", "NWC"),
        feature_group_count=signal.shape[1],
        preferred_element_type=jnp.float32,
    )
    return result[0]


def short_forward(padded, weights, count):
    lag = weights.shape[1] - 1
    result = weights[:, 0][:, None, :] * padded[:, lag : lag + count]
    for offset in range(1, weights.shape[1]):
        result = (
            result + weights[:, offset][:, None, :] * padded[:, lag - offset : lag - offset + count]
        )
    return result


def short_backward(trailing, weights, count):
    result = weights[:, 0][:, None, :] * trailing[:, 0:count]
    for offset in range(1, weights.shape[1]):
        result = result + weights[:, offset][:, None, :] * trailing[:, offset : offset + count]
    return result


def lower_rows(piece):
    return from_behind(piece, "seq", 1)


def upper_rows(piece):
    return from_behind(piece, "seq", -1)


def local(inputs, grad_out, filters, short_weights):
    rows = inputs.shape[1]
    lag = SHORT_LEN - 1
    reach = FILTER_LEN - 1
    taps = lax.all_to_all(filters, "fsdp", split_axis=1, concat_axis=0, tiled=True)
    weights = short_weights.astype(jnp.float32)
    earlier = lower_rows(inputs[:, rows - lag :])
    padded = jnp.concatenate([earlier, inputs], axis=1).astype(jnp.float32)
    shorts = short_forward(padded, weights, rows)
    mixed = (shorts[1] * shorts[2]).astype(jnp.bfloat16)
    mixed_below = lower_rows(mixed[rows - reach :])
    mixed_ext = jnp.concatenate([mixed_below, mixed], axis=0)
    long_out = depthwise(mixed_ext, taps[::-1])
    upstream = grad_out.astype(jnp.float32)
    grad_q = (upstream * long_out).astype(jnp.bfloat16)
    grad_long = (upstream * shorts[0]).astype(jnp.bfloat16)
    following = upper_rows(grad_long[:reach])
    grad_mixed = depthwise(jnp.concatenate([grad_long, following], axis=0), taps)
    grad_k = (grad_mixed * shorts[2]).astype(jnp.bfloat16)
    grad_v = (grad_mixed * shorts[1]).astype(jnp.bfloat16)
    stacked = jnp.stack([grad_q, grad_k, grad_v])
    upper = upper_rows(stacked[:, :lag])
    trailing = jnp.concatenate([stacked, upper], axis=1).astype(jnp.float32)
    grad_inputs = short_backward(trailing, weights, rows).astype(jnp.bfloat16)
    stacked_wide = stacked.astype(jnp.float32)
    short_terms = jnp.stack(
        [
            jnp.sum(stacked_wide * padded[:, lag - offset : lag - offset + rows], axis=1)
            for offset in range(SHORT_LEN)
        ],
        axis=1,
    )
    filter_terms = depthwise(mixed_ext, grad_long)[::-1]
    split_terms = lax.all_to_all(filter_terms, "fsdp", split_axis=0, concat_axis=1, tiled=True)
    grad_filters, grad_short = lax.psum((split_terms, short_terms), "seq")
    return (grad_inputs, grad_filters, grad_short)


def solution(mesh):
    placed = (P(None, "seq", "fsdp"), P("seq", "fsdp"), P("fsdp", None), P(None, None, "fsdp"))
    return jax.shard_map(
        local,
        mesh=mesh,
        in_specs=placed,
        out_specs=(P(None, "seq", "fsdp"), P("fsdp", None), P(None, None, "fsdp")),
        check_vma=False,
    )
```

profile of v0, /device:TPU:0, one launch (start us, length us, event | category | flops | bytes accessed | tf_op | source)
XLA Modules:
  0.0 269.1 jit_solution(8510922553852567944)
XLA Ops:
  8.1 4.9 %collective-permute-start = (bf16[3,2,2048]{2,1,0:T(2,128)(2,1)S(1)}, bf16[3,2,2048]{2,1,0:T(2,128)(2,1)S(1)}, u32[]{:S(2)}, u32[]{:S(2)}) collective-permute-start(bf16[3,2,2048]{2,1,0:T(2,128)(2,1)S(1)} %slice.60), channel_id=1, source_target_pairs={{0,4},{4,8},{8,12},{12,16},{16,20},{20,24},{24,28},{1,5},{5,9},{9,... | collective-permute-start | bytes 73736 | tf_op jit(solution)/shard_map/ppermute | solution.py:13
  14.5 2.8 %maximum_convert_fusion = f32[3,258,2048]{2,1,0:T(8,128)S(1)} fusion(bf16[3,256,2048]{2,1,0:T(8,128)(2,1)} %param.4, bf16[3,2,2048]{2,1,0:T(2,128)(2,1)S(1)} %collective-permute-done), kind=kLoop, calls=%fused_computation.13 | loop fusion | flops 6340608 | bytes 9510912 | tf_op jit(solution)/shard_map/convert_element_type | solution.py:61
  17.4 1.9 multiply_add_fusion
  23.2 4.1 %all-to-all-start = ((bf16[32,4,2048]{2,0,1:T(8,128)(2,1)}), bf16[32,4,2048]{2,0,1:T(8,128)(2,1)}, u32[]{:S(2)}, u32[]{:S(2)}) async-start(bf16[32,4,2048]{2,0,1:T(8,128)(2,1)} %bitcast.43), calls=%async_computation | async-start | bytes 1048576 | tf_op jit(solution)/shard_map/all_to_all | solution.py:58
  27.4 8.2 %collective-permute-done.2 = bf16[127,2048]{1,0:T(8,128)(2,1)} collective-permute-done((bf16[127,2048]{1,0:T(8,128)(2,1)S(1)}, bf16[127,2048]{1,0:T(8,128)(2,1)}, u32[]{:S(2)}, u32[]{:S(2)}) %collective-permute-start.2) | collective-permute-done | bytes 520224 | tf_op jit(solution)/shard_map/ppermute | solution.py:13
  35.6 2.5 maximum_bitcast_fusion.1
  38.1 29.6 %fusion.6 = f32[1,256,2048]{2,0,1:T(1,128)S(1)} fusion(bf16[1,383,2048]{2,1,0:T(8,128)(2,1)} %maximum_bitcast_fusion.1, bf16[128,1,2048]{2,0,1:T(8,128)(2,1)} %bitcast.9), kind=kOutput, calls=%fused_computation.16 | convolution fusion | flops 134217728 | bytes 4190208 | tf_op jit(solution)/shard_map/conv_general_dilated | solution.py:17
  67.7 2.8 %multiply_convert_fusion.1 = (bf16[1,256,2048]{2,1,0:T(8,128)(2,1)}, bf16[1,256,2048]{2,1,0:T(8,128)(2,1)}, bf16[1,256,2048]{2,1,0:T(8,128)(2,1)S(1)}) fusion(f32[3,256,2048]{2,1,0:T(8,128)S(1)} %bitcast.46, f32[1,256,2048]{2,0,1:T(1,128)S(1)} %fusion.6), kind=kLoop, calls=%fused_computation.29 | loop fusion | flops 3145728 | bytes 9437184 | tf_op jit(solution)/shard_map/convert_element_type | solution.py:72
  70.7 5.5 %collective-permute-start.1 = (bf16[127,2048]{1,0:T(8,128)(2,1)S(1)}, bf16[127,2048]{1,0:T(8,128)(2,1)}, u32[]{:S(2)}, u32[]{:S(2)}) collective-permute-start(bf16[127,2048]{1,0:T(8,128)(2,1)S(1)} %slice_bitcast_fusion.1), channel_id=1, source_target_pairs={{0,4},{4,8},{8,12},{12,16},{16,20},{20,24},{24,28},{1,5},{5,9},{9,... | collective-permute-start | bytes 1560584 | tf_op jit(solution)/shard_map/ppermute | solution.py:13
  76.2 6.3 %rev.6 = bf16[128,2048]{1,0:T(8,128)(2,1)S(1)} reverse(bf16[128,2048]{1,0:T(8,128)(2,1)} %bitcast.4), dimensions={0} | reverse | bytes 1048576 | tf_op jit(solution)/shard_map/rev | solution.py:66
  82.5 2.0 collective-permute-done.1
  85.9 27.9 %fusion.8 = f32[1,128,2048]{2,0,1:T(1,128)S(1)} fusion(bf16[1,383,2048]{2,1,0:T(8,128)(2,1)S(1)} %maximum_bitcast_fusion, bf16[256,1,2048]{2,0,1:T(8,128)(2,1)S(1)} %bitcast.48), kind=kOutput, calls=%fused_computation.20 | convolution fusion | flops 134217728 | bytes 3665920 | tf_op jit(solution)/shard_map/conv_general_dilated | solution.py:17
  113.8 28.6 %fusion.10 = f32[1,256,2048]{2,0,1:T(1,128)S(1)} fusion(bf16[1,383,2048]{2,1,0:T(8,128)(2,1)S(1)} %maximum_bitcast_fusion, bf16[128,1,2048]{2,0,1:T(8,128)(2,1)S(1)} %bitcast.53), kind=kOutput, calls=%fused_computation.22 | convolution fusion | flops 134217728 | bytes 4190208 | tf_op jit(solution)/shard_map/conv_general_dilated | solution.py:17
  143.6 1.4 copy.86
  145.0 8.9 %rev.7 = f32[128,2048]{1,0:T(8,128)} reverse(f32[128,2048]{1,0:T(8,128)} %bitcast.51), dimensions={0} | reverse | bytes 2097152 | tf_op jit(solution)/shard_map/rev | solution.py:86
  154.0 4.2 %all-to-all-start.1 = ((f32[4,32,2048]{2,1,0:T(8,128)}), f32[4,32,2048]{2,1,0:T(8,128)}, u32[]{:S(2)}, u32[]{:S(2)}) async-start(f32[4,32,2048]{2,1,0:T(8,128)} %bitcast.50), calls=%async_computation.1 | async-start | bytes 2097152 | tf_op jit(solution)/shard_map/all_to_all | solution.py:87
  158.7 1.5 collective-permute-start.3
  160.1 8.0 %fusion = (f32[3,2048]{1,0:T(4,128)S(1)}, f32[3,2048]{1,0:T(4,128)S(1)}, f32[3,2048]{1,0:T(4,128)S(1)}) fusion(f32[3,258,2048]{2,1,0:T(8,128)} %copy-done, bf16[1,256,2048]{2,1,0:T(8,128)(2,1)S(1)} %copy-done.3, bf16[1,256,2048]{2,1,0:T(8,128)(2,1)S(1)} %copy-done.2, bf16[1,256,2048]{2,1,0:T(8,128)(2,1)S(1)} %fusion.15), kind=kLoop, calls=%fused_computation.3 | loop fusion | flops 14137344 | bytes 22093824 | tf_op jit(solution)/shard_map/reduce_sum | solution.py:81
  168.8 3.9 %all-to-all-done.1 = f32[4,32,2048]{2,1,0:T(8,128)} async-done(((f32[4,32,2048]{2,1,0:T(8,128)}), f32[4,32,2048]{2,1,0:T(8,128)}, u32[]{:S(2)}, u32[]{:S(2)}) %all-to-all-start.1) | async-done | bytes 1048608 | tf_op jit(solution)/shard_map/all_to_all | solution.py:87
  172.7 2.3 copy.63
  175.9 3.2 %fusion.4 = bf16[3,256,2048]{2,1,0:T(8,128)(2,1)} fusion(f32[3,258,2048]{2,1,0:T(8,128)S(1)} %maximum_convert_fusion.1, f32[3,2048]{1,0:T(4,128)S(1)} %copy-done.10, f32[3,2048]{1,0:T(4,128)S(1)} %copy-done.12, f32[3,2048]{1,0:T(4,128)S(1)} %bitcast.55), kind=kLoop, calls=%fused_computation.8 | loop fusion | flops 9437184 | bytes 22093824 | tf_op jit(solution)/shard_map/convert_element_type | solution.py:77
  179.1 79.3 %all-reduce.3.cloned.1.call-done = (f32[32,8192]{1,0:T(8,128)}, f32[3,3,2048]{2,0,1:T(4,128)}) async-done(((f32[32,8192]{1,0:T(8,128)}, f32[3,3,2048]{2,0,1:T(4,128)}), (f32[32,8192]{1,0:T(8,128)}, f32[3,3,2048]{2,0,1:T(4,128)})) %all-reduce.3.cloned.1.call-update) | async-done | bytes 1122320 | tf_op jit(solution)/shard_map/psum | solution.py:88
  258.4 1.6 copy.56
  259.9 2.3 copy.91
  (55 shorter events, 10.7 us)
Async XLA Ops:
  8.1 6.4 %collective-permute-start = (bf16[3,2,2048]{2,1,0:T(2,128)(2,1)S(1)}, bf16[3,2,2048]{2,1,0:T(2,128)(2,1)S(1)}, u32[]{:S(2)}, u32[]{:S(2)}) collective-permute-start(bf16[3,2,2048]{2,1,0:T(2,128)(2,1)S(1)} %slice.60), channel_id=1, source_target_pairs={{0,4},{4,8},{8,12},{12,16},{16,20},{20,24},{24,28},{1,5},{5,9},{9,... | collective-permute-start | bytes 73736 | tf_op jit(solution)/shard_map/ppermute | solution.py:13
  14.0 3.4 %copy-start.9 = (f32[3,2048]{1,0:T(4,128)}, f32[3,2048]{1,0:T(4,128)S(1)}, u32[]{:S(2)}) copy-start(f32[3,2048]{1,0:T(4,128)S(1)} %get-tuple-element.26) | copy-start | bytes 73732
  14.0 3.4 %copy-start.11 = (f32[3,2048]{1,0:T(4,128)}, f32[3,2048]{1,0:T(4,128)S(1)}, u32[]{:S(2)}) copy-start(f32[3,2048]{1,0:T(4,128)S(1)} %get-tuple-element.27) | copy-start | bytes 73732
  14.0 3.3 %copy-start.13 = (f32[3,1,2048]{2,0,1:T(4,128)}, f32[3,1,2048]{2,0,1:T(4,128)S(1)}, u32[]{:S(2)}) copy-start(f32[3,1,2048]{2,0,1:T(4,128)S(1)} %copy.88) | copy-start | bytes 73732
  17.3 2.7 %copy-start = (f32[3,258,2048]{2,1,0:T(8,128)}, f32[3,258,2048]{2,1,0:T(8,128)S(1)}, u32[]{:S(2)}) copy-start(f32[3,258,2048]{2,1,0:T(8,128)S(1)} %maximum_convert_fusion) | copy-start | bytes 19021828
  17.4 2.7 copy-start.6
  20.0 3.2 %copy-start.1 = (f32[3,256,2048]{2,1,0:T(8,128)}, f32[3,256,2048]{2,1,0:T(8,128)S(1)}, u32[]{:S(2)}) copy-start(f32[3,256,2048]{2,1,0:T(8,128)S(1)} %multiply_add_fusion) | copy-start | bytes 18874372
  20.0 1.8 copy-start.8
  20.3 17.8 %copy-start.4 = (bf16[256,2048]{1,0:T(8,128)(2,1)}, bf16[256,2048]{1,0:T(8,128)(2,1)S(1)}, u32[]{:S(2)}) copy-start(bf16[256,2048]{1,0:T(8,128)(2,1)S(1)} %fusion.13) | copy-start | bytes 3145732
  20.4 15.2 %collective-permute-start.2 = (bf16[127,2048]{1,0:T(8,128)(2,1)S(1)}, bf16[127,2048]{1,0:T(8,128)(2,1)}, u32[]{:S(2)}, u32[]{:S(2)}) collective-permute-start(bf16[127,2048]{1,0:T(8,128)(2,1)S(1)} %slice.86), channel_id=1, source_target_pairs={{4,0},{8,4},{12,8},{16,12},{20,16},{24,20},{28,24},{5,1},{9,5},{13... | collective-permute-start | bytes 1560584 | tf_op jit(solution)/shard_map/ppermute | solution.py:13
  23.2 14.9 %all-to-all-start = ((bf16[32,4,2048]{2,0,1:T(8,128)(2,1)}), bf16[32,4,2048]{2,0,1:T(8,128)(2,1)}, u32[]{:S(2)}, u32[]{:S(2)}) async-start(bf16[32,4,2048]{2,0,1:T(8,128)(2,1)} %bitcast.43), calls=%async_computation | async-start | bytes 1048576 | tf_op jit(solution)/shard_map/all_to_all | solution.py:58
  35.6 32.1 %slice-start = ((s8[6291456]{0:T(1024)(128)(4,1)}), s8[2097152]{0:T(1024)(128)(4,1)S(1)}, s32[]{:S(2)}) async-start(s8[6291456]{0:T(1024)(128)(4,1)} %bitcast.45), calls=%async_computation.3 | async-start | bytes 4194304
  38.1 29.6 %slice-start.1 = ((s8[6291456]{0:T(1024)(128)(4,1)}), s8[4194304]{0:T(1024)(128)(4,1)S(1)}, s32[]{:S(2)}) async-start(s8[6291456]{0:T(1024)(128)(4,1)} %bitcast.45), calls=%async_computation.4 | async-start | bytes 8388608
  70.6 15.3 %copy-start.5 = (bf16[256,2048]{1,0:T(8,128)(2,1)S(1)}, bf16[256,2048]{1,0:T(8,128)(2,1)}, u32[]{:S(2)}) copy-start(bf16[256,2048]{1,0:T(8,128)(2,1)} %copy-done.4) | copy-start | bytes 3145732
  70.7 13.8 %collective-permute-start.1 = (bf16[127,2048]{1,0:T(8,128)(2,1)S(1)}, bf16[127,2048]{1,0:T(8,128)(2,1)}, u32[]{:S(2)}, u32[]{:S(2)}) collective-permute-start(bf16[127,2048]{1,0:T(8,128)(2,1)S(1)} %slice_bitcast_fusion.1), channel_id=1, source_target_pairs={{0,4},{4,8},{8,12},{12,16},{16,20},{20,24},{24,28},{1,5},{5,9},{9,... | collective-permute-start | bytes 1560584 | tf_op jit(solution)/shard_map/ppermute | solution.py:13
  113.8 28.7 %copy-start.7 = (bf16[256,2048]{1,0:T(8,128)(2,1)S(1)}, bf16[256,2048]{1,0:T(8,128)(2,1)}, u32[]{:S(2)}) copy-start(bf16[256,2048]{1,0:T(8,128)(2,1)} %param.5) | copy-start | bytes 3145732
  143.6 14.7 %copy-start.2 = (bf16[1,256,2048]{2,1,0:T(8,128)(2,1)S(1)}, bf16[1,256,2048]{2,1,0:T(8,128)(2,1)}, u32[]{:S(2)}) copy-start(bf16[1,256,2048]{2,1,0:T(8,128)(2,1)} %get-tuple-element.20) | copy-start | bytes 3145732
  143.6 14.7 %copy-start.3 = (bf16[1,256,2048]{2,1,0:T(8,128)(2,1)S(1)}, bf16[1,256,2048]{2,1,0:T(8,128)(2,1)}, u32[]{:S(2)}) copy-start(bf16[1,256,2048]{2,1,0:T(8,128)(2,1)} %get-tuple-element.21) | copy-start | bytes 3145732
  154.0 18.7 %all-to-all-start.1 = ((f32[4,32,2048]{2,1,0:T(8,128)}), f32[4,32,2048]{2,1,0:T(8,128)}, u32[]{:S(2)}, u32[]{:S(2)}) async-start(f32[4,32,2048]{2,1,0:T(8,128)} %bitcast.50), calls=%async_computation.1 | async-start | bytes 2097152 | tf_op jit(solution)/shard_map/all_to_all | solution.py:87
  158.2 100.2 %all-reduce.3.cloned.1.call-start = ((), (), s32[]{:S(2)}) async-start(), calls=%async_computation.2 | async-start | bytes 2293760 | tf_op jit(solution)/shard_map/psum | solution.py:88
  158.7 16.4 %collective-permute-start.3 = (bf16[3,2,2048]{2,1,0:T(2,128)(2,1)S(1)}, bf16[3,2,2048]{2,1,0:T(2,128)(2,1)S(1)}, u32[]{:S(2)}, u32[]{:S(2)}) collective-permute-start(bf16[3,2,2048]{2,1,0:T(2,128)(2,1)S(1)} %slice.87), channel_id=1, source_target_pairs={{4,0},{8,4},{12,8},{16,12},{20,16},{24,20},{28,24},{5,1},{9,5},{13... | collective-permute-start | bytes 73736 | tf_op jit(solution)/shard_map/ppermute | solution.py:13
  175.0 0.9 copy-start.10
  175.0 0.9 copy-start.12
  175.0 0.9 copy-start.14
Sparse Core Ops, SparseCore 0:
  175.1 83.1 all-reduce.2
where the time goes:
time: 271 us; the launch traced here: 269 us
  waiting for transfers between devices  93.9 us (35%)
  matrix products  86.2 us (32%)
  local copies, waits for them, and re-layouts  27.1 us (10%)
  other arithmetic  25.7 us (9%)
  starting transfers between devices  21.7 us (8%)
  between operations  14.4 us (5%)
    conv_general_dilated x3, matrix products, depthwise(): lax.conv_general_dilated(signal[None], kernel[:, None, :], (1,), 'VALID',...  86.2 us
    psum x1, waiting for transfers between devices, local(): grad_filters, grad_short = lax.psum((split_terms, short_terms), 'seq')  79.3 us
    ppermute x4, starting transfers between devices, from_behind(): return lax.ppermute(block, axis, route)  13.3 us
    ppermute x4, waiting for transfers between devices, from_behind(): return lax.ppermute(block, axis, route)  10.7 us
    rev x1, local copies, waits for them, and re-layouts, local(): filter_terms = depthwise(mixed_ext, grad_long)[::-1]  8.92 us
    reduce_sum x1, other arithmetic, local(): jnp.sum(stacked_wide * padded[:, lag - offset:lag - offset + rows], axis=1)  8.03 us
    rev x1, local copies, waits for them, and re-layouts, local(): long_out = depthwise(mixed_ext, taps[::-1])  6.31 us
    unnamed x39, local copies, waits for them, and re-layouts  6.15 us
  transfers between devices with their start and end apart: 7, of which 5 were waited for; matrix products, arithmetic and copies ran while one was open for 10% of the time, Pallas kernels for 0%

commit v1 on v0

v1 whole, which is shorter than its diff:
```python
import functools

import jax
import jax.numpy as jnp
import numpy as np
from jax import lax
from jax.experimental import pallas as pl
from jax.experimental.pallas import tpu as pltpu
from jax.sharding import PartitionSpec as P

BF16 = jnp.bfloat16
F32 = jnp.float32


def dft_matrices(count):
    angle = np.arange(count)[None, :] * (np.arange(count // 2)[:, None] + 0.5) * (2 * np.pi / count)
    forward = np.concatenate([np.cos(angle), -np.sin(angle)], axis=0)
    backward = forward.T * (2.0 / count)
    return forward, backward


def split(matrix):
    high = matrix.astype(BF16)
    low = (matrix - high.astype(np.float64)).astype(BF16)
    return high, low


def dot(a, b):
    return jnp.dot(a, b, preferred_element_type=F32)


def forward(mat, signal):
    return dot(mat[0], signal) + dot(mat[1], signal)


def inverse(mat, spectrum):
    high = spectrum.astype(BF16)
    low = (spectrum - high.astype(F32)).astype(BF16)
    return dot(mat[0], high) + dot(mat[1], high) + dot(mat[0], low)


def times(a, b):
    half = a.shape[0] // 2
    ar, ai, br, bi = a[:half], a[half:], b[:half], b[half:]
    return jnp.concatenate([ar * br - ai * bi, ar * bi + ai * br], axis=0)


def times_conj(a, b):
    half = a.shape[0] // 2
    ar, ai, br, bi = a[:half], a[half:], b[:half], b[half:]
    return jnp.concatenate([ar * br + ai * bi, ai * br - ar * bi], axis=0)


def delayed(x, before):
    row = lax.broadcasted_iota(jnp.int32, x.shape, 0)
    older, newer = before[0:1], before[1:2]
    one = jnp.where(row == 0, newer, pltpu.roll(x, 1, 0))
    two = jnp.where(row == 0, older, jnp.where(row == 1, newer, pltpu.roll(x, 2, 0)))
    return x, one, two


def advanced(x):
    rows = x.shape[0]
    row = lax.broadcasted_iota(jnp.int32, x.shape, 0)
    one = jnp.where(row == rows - 1, 0.0, pltpu.roll(x, rows - 1, 0))
    two = jnp.where(row >= rows - 2, 0.0, pltpu.roll(x, rows - 2, 0))
    return x, one, two


def weighted(terms, weights, i):
    out = weights[i, 0:1] * terms[0]
    for j in range(1, len(terms)):
        out = out + weights[i, j : j + 1] * terms[j]
    return out


def tail_body(near_ref, last_ref, w_ref, out_ref):
    w = w_ref[...].astype(F32)
    lead = near_ref.shape[1]
    shorts = []
    for i in (1, 2):
        x = last_ref[i - 1].astype(F32)
        before = near_ref[i - 1].astype(F32)[lead - 2 :]
        shorts.append(weighted(delayed(x, before), w, i))
    out_ref[...] = (shorts[0] * shorts[1]).astype(BF16)


def local_body(x_ref, before_ref, go_ref, w_ref, taps_ref, fh_ref, fl_ref, head_ref, a_ref, g_ref, h_ref):
    w = w_ref[...].astype(F32)
    rows = go_ref.shape[0]
    reach = taps_ref.shape[0]
    q, k, v = [
        weighted(delayed(x_ref[i].astype(F32), before_ref[i].astype(F32)), w, i) for i in range(3)
    ]
    mixed = (k * v).astype(BF16)
    grad_long = (go_ref[...].astype(F32) * q).astype(BF16)
    head_ref[...] = grad_long[:reach]
    a_ref[...] = forward((fh_ref[:, reach:], fl_ref[:, reach:]), mixed)
    g_ref[...] = forward((fh_ref[:, :rows], fl_ref[:, :rows]), grad_long)
    h_ref[...] = forward((fh_ref[:, :reach], fl_ref[:, :reach]), taps_ref[...])


def filter_body(halo_ref, a_ref, g_ref, fh_ref, fl_ref, bh_ref, bl_ref, full_ref, out_ref):
    full = a_ref[...] + forward((fh_ref[...], fl_ref[...]), halo_ref[...])
    full_ref[...] = full
    out_ref[...] = inverse((bh_ref[...], bl_ref[...]), times_conj(full, g_ref[...]))


def output_body(
    x_ref, before_ref, go_ref, w_ref, next_ref, a_ref, g_ref, h_ref, fh_ref, fl_ref, bh_ref, bl_ref,
    gi_ref, tail_ref, first_ref, short_ref,
):
    w = w_ref[...].astype(F32)
    rows = go_ref.shape[0]
    reach = next_ref.shape[0]
    h = h_ref[...]
    long_out = inverse((bh_ref[reach:], bl_ref[reach:]), times(a_ref[...], h))
    g = g_ref[...] + forward((fh_ref[...], fl_ref[...]), next_ref[...])
    grad_mixed = inverse((bh_ref[:rows], bl_ref[:rows]), times_conj(g, h))
    shifted = [delayed(x_ref[i].astype(F32), before_ref[i].astype(F32)) for i in range(3)]
    k, v = weighted(shifted[1], w, 1), weighted(shifted[2], w, 2)
    grads = (go_ref[...].astype(F32) * long_out, grad_mixed * v, grad_mixed * k)
    for i in range(3):
        low = grads[i].astype(BF16)
        first_ref[i] = low[:2]
        wide = low.astype(F32)
        result = weighted(advanced(wide), w, i)
        tail_ref[i] = result[rows - 2 :]
        gi_ref[i] = result.astype(BF16)
        for j in range(3):
            short_ref[i, j : j + 1] = jnp.sum(wide * shifted[i][j], axis=0, keepdims=True)


def finish_body(old_ref, tail_ref, next_ref, w_ref, out_ref):
    w = w_ref[...].astype(F32)
    rows = old_ref.shape[1]
    row = lax.broadcasted_iota(jnp.int32, old_ref.shape[1:], 0)
    for i in range(3):
        after = next_ref[i].astype(F32)
        part = tail_ref[i]
        one = part[0:1] + w[i, 2:3] * after[0:1]
        two = part[1:2] + w[i, 1:2] * after[0:1] + w[i, 2:3] * after[1:2]
        old = old_ref[i].astype(F32)
        new = jnp.where(row == rows - 2, one, jnp.where(row == rows - 1, two, old))
        out_ref[i] = new.astype(BF16)


def exchange(block, axis, flip):
    return lax.ppermute(block, axis, [(i, i ^ flip) for i in range(lax.axis_size(axis))])


def shift(block, axis, distance):
    count = lax.axis_size(axis)
    return lax.ppermute(
        block, axis, [(i, i + distance) for i in range(count) if 0 <= i + distance < count]
    )


def pick(stacked, index):
    return lax.dynamic_index_in_dim(stacked, index, 0, keepdims=False)


def reduce_filters(terms, parts):
    seq, fsdp = lax.axis_size("seq"), lax.axis_size("fsdp")
    taps, channels = terms.shape
    if seq & (seq - 1) or fsdp & (fsdp - 1) or channels % (128 * seq) or seq < 2 or seq > 16:
        pieces = lax.all_to_all(terms, "fsdp", split_axis=0, concat_axis=1, tiled=True)
        return lax.psum(pieces, "seq")
    me, mine = lax.axis_index("seq"), lax.axis_index("fsdp")
    width = channels // seq
    pairs = seq // 2
    by_owner = terms.reshape(taps, pairs, 2, width).transpose(2, 1, 0, 3)
    side = me % 2
    keep, give = pick(by_owner, side), pick(by_owner, 1 - side)
    keep = keep + exchange(give.astype(BF16), "seq", 1).astype(F32)
    place = me // 2
    own = pick(keep, place)
    for flip in range(1, pairs):
        own = own + exchange(pick(keep, place ^ flip).astype(BF16), "seq", 2 * flip).astype(F32)
    blocks = own.astype(BF16).reshape(fsdp, taps // fsdp, width)
    wanted = jnp.zeros((fsdp, taps // fsdp, width), BF16)
    wanted = lax.dynamic_update_index_in_dim(wanted, pick(blocks, mine), mine, 0)
    for flip in range(1, fsdp):
        got = exchange(pick(blocks, mine ^ flip), "fsdp", flip)
        wanted = lax.dynamic_update_index_in_dim(wanted, got, mine ^ flip, 0)
    pieces = [wanted] + [exchange(wanted, "seq", 2 * flip) for flip in range(1, pairs)]
    others = [exchange(piece, "seq", 1) for piece in pieces]
    whole = jnp.zeros((seq, fsdp, taps // fsdp, width), BF16)
    for flip in range(pairs):
        whole = lax.dynamic_update_index_in_dim(whole, pieces[flip], me ^ (2 * flip), 0)
        whole = lax.dynamic_update_index_in_dim(whole, others[flip], me ^ (2 * flip) ^ 1, 0)
    return whole.transpose(2, 1, 0, 3).reshape(taps // fsdp, fsdp * channels).astype(F32)


def reduce_short(terms):
    seq = lax.axis_size("seq")
    if seq & (seq - 1):
        return lax.psum(terms, "seq")
    flip = 1
    while flip < seq:
        terms = terms + exchange(terms, "seq", flip)
        flip *= 2
    return terms


def local(inputs, grad_out, filters, short_weights):
    kinds, rows, channels = inputs.shape
    lag = short_weights.shape[1] - 1
    fsdp = lax.axis_size("fsdp")
    reach = filters.shape[0] * fsdp
    count = rows + reach
    fwd, bwd = dft_matrices(count)
    fh, fl = [jnp.asarray(m) for m in split(fwd)]
    bh, bl = [jnp.asarray(m) for m in split(bwd)]
    width = 256 if channels % 256 == 0 else channels
    grid = (channels // width,)
    near = 16

    def cols(*lead):
        return pl.BlockSpec((*lead, width), lambda c: (*([0] * len(lead)), c))

    def whole(shape):
        return pl.BlockSpec(shape, lambda c: (0, 0))

    def sds(shape, dtype):
        return jax.ShapeDtypeStruct(shape, dtype)

    w_spec = cols(kinds, lag + 1)
    before = shift(inputs[:, rows - lag :], "seq", 1)
    skip = rows - reach
    pair = inputs[1:]
    tail = pl.pallas_call(
        tail_body,
        grid=grid,
        in_specs=[
            pl.BlockSpec((2, near, width), lambda c: (0, skip // near - 1, c)),
            pl.BlockSpec((2, reach, width), lambda c: (0, skip // reach, c)),
            w_spec,
        ],
        out_specs=cols(reach),
        out_shape=sds((reach, channels), BF16),
        name="tail",
    )(pair, pair, short_weights)
    halo = shift(tail, "seq", 1)
    taps = lax.all_to_all(filters, "fsdp", split_axis=1, concat_axis=0, tiled=True)

    head, a_local, g_local, h = pl.pallas_call(
        local_body,
        grid=grid,
        in_specs=[cols(kinds, rows), cols(kinds, lag), cols(rows), w_spec, cols(reach)]
        + [whole((count, count))] * 2,
        out_specs=[cols(reach), cols(count), cols(count), cols(count)],
        out_shape=[sds((reach, channels), BF16)] + [sds((count, channels), F32)] * 3,
        name="local",
    )(inputs, before, grad_out, short_weights, taps, fh, fl)

    order = reach - np.arange(reach)
    a_full, terms = pl.pallas_call(
        filter_body,
        grid=grid,
        in_specs=[cols(reach), cols(count), cols(count)]
        + [whole((count, reach))] * 2
        + [whole((reach, count))] * 2,
        out_specs=[cols(count), cols(reach)],
        out_shape=[sds((count, channels), F32), sds((reach, channels), F32)],
        name="filters",
    )(halo, a_local, g_local, fh[:, :reach], fl[:, :reach], bh[order], bl[order])
    grad_filters = reduce_filters(terms, None)

    following = shift(head, "seq", -1)
    partial, tails, firsts, shorts = pl.pallas_call(
        output_body,
        grid=grid,
        in_specs=[
            cols(kinds, rows), cols(kinds, lag), cols(rows), w_spec, cols(reach),
            cols(count), cols(count), cols(count),
        ]
        + [whole((count, reach))] * 2
        + [whole((count, count))] * 2,
        out_specs=[cols(kinds, rows), cols(kinds, lag), cols(kinds, lag), cols(kinds, lag + 1)],
        out_shape=[
            sds((kinds, rows, channels), BF16),
            sds((kinds, lag, channels), F32),
            sds((kinds, lag, channels), BF16),
            sds((kinds, lag + 1, channels), F32),
        ],
        name="outputs",
    )(
        inputs, before, grad_out, short_weights, following, a_full, g_local, h,
        fh[:, rows:], fl[:, rows:], bh, bl,
    )
    grad_short = reduce_short(shorts)
    after = shift(firsts, "seq", -1)
    last = pl.BlockSpec((kinds, near, width), lambda c: (0, rows // near - 1, c))
    grad_inputs = pl.pallas_call(
        finish_body,
        grid=grid,
        in_specs=[last, cols(kinds, lag), cols(kinds, lag), w_spec],
        out_specs=last,
        out_shape=sds((kinds, rows, channels), BF16),
        input_output_aliases={0: 0},
        name="finish",
    )(partial, tails, after, short_weights)
    return (grad_inputs, grad_filters, grad_short)


def solution(mesh):
    placed = (P(None, "seq", "fsdp"), P("seq", "fsdp"), P("fsdp", None), P(None, None, "fsdp"))
    return jax.shard_map(
        local,
        mesh=mesh,
        in_specs=placed,
        out_specs=(P(None, "seq", "fsdp"), P("fsdp", None), P(None, None, "fsdp")),
        check_vma=False,
    )
```

time: 271 us -> 132 us (0.49)
  matrix products: 86.2 us -> 0 us
  waiting for transfers between devices: 93.9 us -> 29.8 us
  Pallas kernels: 0 us -> 46.5 us
  other arithmetic: 25.7 us -> 0.97 us
  starting transfers between devices: 21.7 us -> 37.5 us
  between operations: 14.4 us -> 1.01 us
  local copies, waits for them, and re-layouts: 27.1 us -> 14.9 us
    conv_general_dilated x3 -> x0, matrix products: 86.2 us -> none  [depthwise(): lax.conv_general_dilated(signal[None], kernel[:, None, :], (1,), 'VALID',...]
    psum x1 -> x0, waiting for transfers between devices: 79.3 us -> none  [local(): grad_filters, grad_short = lax.psum((split_terms, short_terms), 'seq')]
    pallas_call x0 -> x5, Pallas kernels: none -> 46.5 us  [the longest x1 17.4 us: local(): pl.pallas_call(output_body, grid=grid, in_specs=[cols(kinds, rows), cols(...]
    ppermute x4 -> x21, starting transfers between devices: 13.3 us -> 34 us  [the longest x17 23.1 us: exchange(): lax.ppermute(block, axis, [(i, i ^ flip) for i in range(lax.axis_size(axi...]
    ppermute x4 -> x21, waiting for transfers between devices: 10.7 us -> 28.5 us  [the longest x17 21.9 us: exchange(): lax.ppermute(block, axis, [(i, i ^ flip) for i in range(lax.axis_size(axi...]
    rev x2 -> x0, local copies, waits for them, and re-layouts: 15.2 us -> none  [the longest x1 8.92 us: local(): filter_terms = depthwise(mixed_ext, grad_long)[::-1]]
    convert_element_type x5 -> x2, other arithmetic: 9.95 us -> 0.14 us  [the longest x1 0.11 us: reduce_filters(): whole.transpose(2, 1, 0, 3).reshape(taps // fsdp, fsdp * channels)]
    reduce_sum x1 -> x0, other arithmetic: 8.03 us -> none  [local(): jnp.sum(stacked_wide * padded[:, lag - offset:lag - offset + rows], axis=1)]
  transfers between devices with their start and end apart: 7 -> 22, of which waited for: 5 -> 11; matrix products, arithmetic and copies ran while one was open for 10% -> 5% of each run, Pallas kernels for 0% -> 24%
where the time goes in v1:
time: 132 us; the launch traced here: 131 us
  Pallas kernels  46.5 us (35%)
  starting transfers between devices  37.5 us (28%)
  waiting for transfers between devices  29.8 us (23%)
  local copies, waits for them, and re-layouts  14.9 us (11%)
    ppermute x17, starting transfers between devices, exchange(): lax.ppermute(block, axis, [(i, i ^ flip) for i in range(lax.axis_size(axi...  23.1 us
    ppermute x17, waiting for transfers between devices, exchange(): lax.ppermute(block, axis, [(i, i ^ flip) for i in range(lax.axis_size(axi...  21.9 us
    pallas_call x1, Pallas kernels, local(): pl.pallas_call(output_body, grid=grid, in_specs=[cols(kinds, rows), cols(...  17.4 us
    ppermute x4, starting transfers between devices, shift(): lax.ppermute(block, axis, [(i, i + distance) for i in range(count) if 0 <...  10.9 us
    pallas_call x1, Pallas kernels, local(): pl.pallas_call(local_body, grid=grid, in_specs=[cols(kinds, rows), cols(k...  9.92 us
    pallas_call x1, Pallas kernels, local(): pl.pallas_call(filter_body, grid=grid, in_specs=[cols(reach), cols(count)...  9.27 us
    ppermute x4, waiting for transfers between devices, shift(): lax.ppermute(block, axis, [(i, i + distance) for i in range(count) if 0 <...  6.66 us
    pallas_call x1, Pallas kernels, local(): pl.pallas_call(tail_body, grid=grid, in_specs=[pl.BlockSpec((2, near, wid...  5.56 us
  transfers between devices with their start and end apart: 22, of which 11 were waited for; matrix products, arithmetic and copies ran while one was open for 5% of the time, Pallas kernels for 24%

profile of v1, /device:TPU:0, one launch (start us, length us, event | category | flops | bytes accessed | tf_op | source)
XLA Modules:
  0.0 130.6 jit_solution(10716116006977460196)
XLA Ops:
  0.6 3.2 %slice.19.near_ref.last_ref = bf16[2,256,2048]{2,1,0:T(8,128)(2,1)} slice(bf16[3,256,2048]{2,1,0:T(8,128)(2,1)} %x_ref.3), slice={[1:3], [0:256], [0:2048]} | slice | bytes 4194304 | tf_op jit(solution)/shard_map/slice | solution.py:231
  3.8 5.6 %tail.1 = bf16[128,2048]{1,0:T(8,128)(2,1)} custom-call(bf16[2,256,2048]{2,1,0:T(8,128)(2,1)} %slice.19.near_ref.last_ref, bf16[2,256,2048]{2,1,0:T(8,128)(2,1)} %slice.19.near_ref.last_ref, bf16[3,3,2048]{2,1,0:T(4,128)(2,1)} %w_ref.7), custom_call_target="tpu_custom_call" | custom-call | tf_op jit(solution)/shard_map/tail/pallas_call | solution.py:232
  9.4 4.9 %collective-permute-start.2 = (bf16[128,2048]{1,0:T(8,128)(2,1)}, bf16[128,2048]{1,0:T(8,128)(2,1)S(1)}, u32[]{:S(2)}, u32[]{:S(2)}) collective-permute-start(bf16[128,2048]{1,0:T(8,128)(2,1)} %tail.1), channel_id=1, source_target_pairs={{0,4},{4,8},{8,12},{12,16},{16,20},{20,24},{24,28},{1,5},{5,9},{9,... | collective-permute-start | bytes 1572872 | tf_op jit(solution)/shard_map/ppermute | solution.py:154
  15.1 3.5 %all-to-all-start = ((bf16[32,4,2048]{2,0,1:T(8,128)(2,1)}), bf16[32,4,2048]{2,0,1:T(8,128)(2,1)S(1)}, u32[]{:S(2)}, u32[]{:S(2)}) async-start(bf16[32,4,2048]{2,0,1:T(8,128)(2,1)} %bitcast.62), calls=%async_computation | async-start | bytes 1048576 | tf_op jit(solution)/shard_map/all_to_all | solution.py:245
  19.5 3.4 %collective-permute-start = (bf16[3,2,2048]{2,1,0:T(2,128)(2,1)S(1)}, bf16[3,2,2048]{2,1,0:T(2,128)(2,1)S(1)}, u32[]{:S(2)}, u32[]{:S(2)}) collective-permute-start(bf16[3,2,2048]{2,1,0:T(2,128)(2,1)S(1)} %slice.18), channel_id=1, source_target_pairs={{0,4},{4,8},{8,12},{12,16},{16,20},{20,24},{24,28},{1,5},{5,9},{9,... | collective-permute-start | bytes 73736 | tf_op jit(solution)/shard_map/ppermute | solution.py:154
  23.0 3.2 %collective-permute-done.before_ref = bf16[3,2,2048]{2,1,0:T(2,128)(2,1)S(1)} collective-permute-done((bf16[3,2,2048]{2,1,0:T(2,128)(2,1)S(1)}, bf16[3,2,2048]{2,1,0:T(2,128)(2,1)S(1)}, u32[]{:S(2)}, u32[]{:S(2)}) %collective-permute-start) | collective-permute-done | bytes 24608 | tf_op jit(solution)/shard_map/ppermute | solution.py:154
  28.1 9.9 %local.1 = (bf16[128,2048]{1,0:T(8,128)(2,1)}, f32[384,2048]{1,0:T(8,128)}, f32[384,2048]{1,0:T(8,128)}, f32[384,2048]{1,0:T(8,128)}) custom-call(bf16[3,256,2048]{2,1,0:T(8,128)(2,1)} %x_ref.3, bf16[3,2,2048]{2,1,0:T(2,128)(2,1)} %copy-done.4, bf16[256,2048]{1,0:T(8,128)(2,1)} %go_ref.3, bf16[3,3,2048]{2,1,0:T(4,128)(2,1)} %w_ref.7, ...), custom_call_target="tpu_custom_call" | custom-call | tf_op jit(solution)/shard_map/local/pallas_call | solution.py:247
  38.9 9.3 %filters.1 = (f32[384,2048]{1,0:T(8,128)}, f32[128,2048]{1,0:T(8,128)}) custom-call(bf16[128,2048]{1,0:T(8,128)(2,1)} %copy-done.2, f32[384,2048]{1,0:T(8,128)} %get-tuple-element.14.a_ref, f32[384,2048]{1,0:T(8,128)} %get-tuple-element.15.g_ref, bf16[384,128]{1,0:T(8,128)(2,1)} %constant.119.fh_ref, bf16[384,128]{1,0:T(8,128)(2,1)} %constant.120.fl_ref, ...), custom_call_target="tpu_custom_call" | custom-call | tf_op jit(solution)/shard_map/filters/pallas_call | solution.py:258
  48.2 2.1 %reshape.22 = f32[128,4,2,256]{3,2,1,0:T(2,128)S(1)} reshape(f32[128,2048]{1,0:T(8,128)} %get-tuple-element.21) | data formatting | bytes 2097152 | tf_op jit(solution)/shard_map/reshape | solution.py:172
  53.0 5.7 %collective-permute-done.4 = bf16[4,128,256]{2,1,0:T(8,128)(2,1)S(1)} collective-permute-done((bf16[4,128,256]{2,1,0:T(8,128)(2,1)S(1)}, bf16[4,128,256]{2,1,0:T(8,128)(2,1)S(1)}, u32[]{:S(2)}, u32[]{:S(2)}) %collective-permute-start.4) | collective-permute-done | bytes 262176 | tf_op jit(solution)/shard_map/ppermute | solution.py:149
  60.6 2.5 %collective-permute-start.6 = (bf16[128,256]{1,0:T(8,128)(2,1)S(1)}, bf16[128,256]{1,0:T(8,128)(2,1)S(1)}, u32[]{:S(2)}, u32[]{:S(2)}) collective-permute-start(bf16[128,256]{1,0:T(8,128)(2,1)S(1)} %get-tuple-element.25), channel_id=1, source_target_pairs={{0,16},{4,20},{8,24},{12,28},{16,0},{20,4},{24,8},{28,12},{1,17},{... | collective-permute-start | bytes 196616 | tf_op jit(solution)/shard_map/ppermute | solution.py:149
  63.3 3.9 %collective-permute-done.6 = bf16[128,256]{1,0:T(8,128)(2,1)S(1)} collective-permute-done((bf16[128,256]{1,0:T(8,128)(2,1)S(1)}, bf16[128,256]{1,0:T(8,128)(2,1)S(1)}, u32[]{:S(2)}, u32[]{:S(2)}) %collective-permute-start.6) | collective-permute-done | bytes 65568 | tf_op jit(solution)/shard_map/ppermute | solution.py:149
  67.2 2.1 %collective-permute-done.7 = bf16[128,256]{1,0:T(8,128)(2,1)S(1)} collective-permute-done((bf16[128,256]{1,0:T(8,128)(2,1)S(1)}, bf16[128,256]{1,0:T(8,128)(2,1)S(1)}, u32[]{:S(2)}, u32[]{:S(2)}) %collective-permute-start.7) | collective-permute-done | bytes 65568 | tf_op jit(solution)/shard_map/ppermute | solution.py:149
  72.6 1.9 %collective-permute-done.9 = bf16[32,256]{1,0:T(8,128)(2,1)S(1)} collective-permute-done((bf16[32,256]{1,0:T(8,128)(2,1)S(1)}, bf16[32,256]{1,0:T(8,128)(2,1)S(1)}, u32[]{:S(2)}, u32[]{:S(2)}) %collective-permute-start.9) | collective-permute-done | bytes 16416 | tf_op jit(solution)/shard_map/ppermute | solution.py:149
  75.5 2.8 %collective-permute-start.11 = (bf16[4,32,256]{2,1,0:T(8,128)(2,1)S(1)}, bf16[4,32,256]{2,1,0:T(8,128)(2,1)S(1)}, u32[]{:S(2)}, u32[]{:S(2)}) collective-permute-start(bf16[4,32,256]{2,1,0:T(8,128)(2,1)S(1)} %bitcast_dynamic-update-slice_fusion.7), channel_id=1, source_target_pairs={{0,4},{4,0},{8,12},{12,8},{16,20},{20,16},{24,28},{28,24},{1,5},{5... | collective-permute-start | bytes 196616 | tf_op jit(solution)/shard_map/ppermute | solution.py:149
  79.7 3.0 %collective-permute-start.16 = (bf16[4,32,256]{2,1,0:T(8,128)(2,1)S(1)}, bf16[4,32,256]{2,1,0:T(8,128)(2,1)S(1)}, u32[]{:S(2)}, u32[]{:S(2)}) collective-permute-start(bf16[4,32,256]{2,1,0:T(8,128)(2,1)S(1)} %bitcast_dynamic-update-slice_fusion.7), channel_id=1, source_target_pairs={{0,24},{4,28},{8,16},{12,20},{16,8},{20,12},{24,0},{28,4},{1,25},{... | collective-permute-start | bytes 196616 | tf_op jit(solution)/shard_map/ppermute | solution.py:149
  82.7 3.4 %collective-permute-done.1.next_ref = bf16[128,2048]{1,0:T(8,128)(2,1)S(1)} collective-permute-done((bf16[128,2048]{1,0:T(8,128)(2,1)S(1)}, bf16[128,2048]{1,0:T(8,128)(2,1)S(1)}, u32[]{:S(2)}, u32[]{:S(2)}) %collective-permute-start.1) | collective-permute-done | bytes 524320 | tf_op jit(solution)/shard_map/ppermute | solution.py:154
  86.9 17.4 %outputs.1 = (bf16[3,256,2048]{2,1,0:T(8,128)(2,1)}, f32[3,2,2048]{2,1,0:T(2,128)}, bf16[3,2,2048]{2,1,0:T(2,128)(2,1)}, f32[3,3,2048]{2,1,0:T(4,128)}) custom-call(bf16[3,256,2048]{2,1,0:T(8,128)(2,1)} %x_ref.3, bf16[3,2,2048]{2,1,0:T(2,128)(2,1)} %copy-done.4, bf16[256,2048]{1,0:T(8,128)(2,1)} %go_ref.3, bf16[3,3,2048]{2,1,0:T(4,128)(2,1)} %w_ref.7, ...), custom_call_target="tpu_custom_call" | custom-call | tf_op jit(solution)/shard_map/outputs/pallas_call | solution.py:271
  104.3 3.1 %collective-permute-start.18 = (f32[3,3,2048]{2,1,0:T(4,128)}, f32[3,3,2048]{2,1,0:T(4,128)S(1)}, u32[]{:S(2)}, u32[]{:S(2)}) collective-permute-start(f32[3,3,2048]{2,1,0:T(4,128)} %get-tuple-element.22), channel_id=1, source_target_pairs={{0,4},{4,0},{8,12},{12,8},{16,20},{20,16},{24,28},{28,24},{1,5},{5... | collective-permute-start | bytes 221192 | tf_op jit(solution)/shard_map/ppermute | solution.py:149
  108.7 2.7 %collective-permute-start.13 = (bf16[4,32,256]{2,1,0:T(8,128)(2,1)S(1)}, bf16[4,32,256]{2,1,0:T(8,128)(2,1)S(1)}, u32[]{:S(2)}, u32[]{:S(2)}) collective-permute-start(bf16[4,32,256]{2,1,0:T(8,128)(2,1)S(1)} %collective-permute-done.12), channel_id=1, source_target_pairs={{0,4},{4,0},{8,12},{12,8},{16,20},{20,16},{24,28},{28,24},{1,5},{5... | collective-permute-start | bytes 196616 | tf_op jit(solution)/shard_map/ppermute | solution.py:149
  111.5 1.9 %collective-permute-start.17 = (bf16[4,32,256]{2,1,0:T(8,128)(2,1)S(1)}, bf16[4,32,256]{2,1,0:T(8,128)(2,1)S(1)}, u32[]{:S(2)}, u32[]{:S(2)}) collective-permute-start(bf16[4,32,256]{2,1,0:T(8,128)(2,1)S(1)} %collective-permute-done.16), channel_id=1, source_target_pairs={{0,4},{4,0},{8,12},{12,8},{16,20},{20,16},{24,28},{28,24},{1,5},{5... | collective-permute-start | bytes 196616 | tf_op jit(solution)/shard_map/ppermute | solution.py:149
  114.2 4.4 %finish.1 = bf16[3,256,2048]{2,1,0:T(8,128)(2,1)} custom-call(bf16[3,256,2048]{2,1,0:T(8,128)(2,1)} %get-tuple-element.18.old_ref, f32[3,2,2048]{2,1,0:T(2,128)} %get-tuple-element.19.tail_ref, bf16[3,2,2048]{2,1,0:T(2,128)(2,1)} %copy-done.6, bf16[3,3,2048]{2,1,0:T(4,128)(2,1)} %w_ref.7), custom_call_target="tpu_custom_call", output_to_operand_aliasing={{}: (0, {})} | custom-call | tf_op jit(solution)/shard_map/finish/pallas_call | solution.py:295
  118.7 4.5 %collective-permute-done.19 = f32[3,3,2048]{2,1,0:T(4,128)S(1)} collective-permute-done((f32[3,3,2048]{2,1,0:T(4,128)S(1)}, f32[3,3,2048]{2,1,0:T(4,128)S(1)}, u32[]{:S(2)}, u32[]{:S(2)}) %collective-permute-start.19) | collective-permute-done | bytes 73760 | tf_op jit(solution)/shard_map/ppermute | solution.py:149
  127.2 2.8 %collective-permute-done.20 = f32[3,3,2048]{2,1,0:T(4,128)S(1)} collective-permute-done((f32[3,3,2048]{2,1,0:T(4,128)S(1)}, f32[3,3,2048]{2,1,0:T(4,128)S(1)}, u32[]{:S(2)}, u32[]{:S(2)}) %collective-permute-start.20) | collective-permute-done | bytes 73760 | tf_op jit(solution)/shard_map/ppermute | solution.py:149
  (72 shorter events, 22.6 us)
Async XLA Ops:
  3.8 10.5 %copy-start.3 = (bf16[32,8192]{1,0:T(8,128)(2,1)S(1)}, bf16[32,8192]{1,0:T(8,128)(2,1)}, u32[]{:S(2)}) copy-start(bf16[32,8192]{1,0:T(8,128)(2,1)} %param.13) | copy-start | bytes 1572868
  9.4 28.7 %collective-permute-start.2 = (bf16[128,2048]{1,0:T(8,128)(2,1)}, bf16[128,2048]{1,0:T(8,128)(2,1)S(1)}, u32[]{:S(2)}, u32[]{:S(2)}) collective-permute-start(bf16[128,2048]{1,0:T(8,128)(2,1)} %tail.1), channel_id=1, source_target_pairs={{0,4},{4,8},{8,12},{12,16},{16,20},{20,24},{24,28},{1,5},{5,9},{9,... | collective-permute-start | bytes 1572872 | tf_op jit(solution)/shard_map/ppermute | solution.py:154
  15.1 12.3 %all-to-all-start = ((bf16[32,4,2048]{2,0,1:T(8,128)(2,1)}), bf16[32,4,2048]{2,0,1:T(8,128)(2,1)S(1)}, u32[]{:S(2)}, u32[]{:S(2)}) async-start(bf16[32,4,2048]{2,0,1:T(8,128)(2,1)} %bitcast.62), calls=%async_computation | async-start | bytes 1048576 | tf_op jit(solution)/shard_map/all_to_all | solution.py:245
  19.5 6.6 %collective-permute-start = (bf16[3,2,2048]{2,1,0:T(2,128)(2,1)S(1)}, bf16[3,2,2048]{2,1,0:T(2,128)(2,1)S(1)}, u32[]{:S(2)}, u32[]{:S(2)}) collective-permute-start(bf16[3,2,2048]{2,1,0:T(2,128)(2,1)S(1)} %slice.18), channel_id=1, source_target_pairs={{0,4},{4,8},{8,12},{12,16},{16,20},{20,24},{24,28},{1,5},{5,9},{9,... | collective-permute-start | bytes 73736 | tf_op jit(solution)/shard_map/ppermute | solution.py:154
  50.3 19.1 %copy-start.7 = (bf16[128,2048]{1,0:T(8,128)(2,1)S(1)}, bf16[128,2048]{1,0:T(8,128)(2,1)}, u32[]{:S(2)}) copy-start(bf16[128,2048]{1,0:T(8,128)(2,1)} %get-tuple-element.13) | copy-start | bytes 1572868
  50.9 7.8 %collective-permute-start.4 = (bf16[4,128,256]{2,1,0:T(8,128)(2,1)S(1)}, bf16[4,128,256]{2,1,0:T(8,128)(2,1)S(1)}, u32[]{:S(2)}, u32[]{:S(2)}) collective-permute-start(bf16[4,128,256]{2,1,0:T(8,128)(2,1)S(1)} %bitcast.68), channel_id=1, source_target_pairs={{0,4},{4,0},{8,12},{12,8},{16,20},{20,16},{24,28},{28,24},{1,5},{5... | collective-permute-start | bytes 786440 | tf_op jit(solution)/shard_map/ppermute | solution.py:149
  58.8 4.5 %collective-permute-start.5 = (bf16[128,256]{1,0:T(8,128)(2,1)S(1)}, bf16[128,256]{1,0:T(8,128)(2,1)S(1)}, u32[]{:S(2)}, u32[]{:S(2)}) collective-permute-start(bf16[128,256]{1,0:T(8,128)(2,1)S(1)} %get-tuple-element.23), channel_id=1, source_target_pairs={{0,8},{4,12},{8,0},{12,4},{16,24},{20,28},{24,16},{28,20},{1,9},{5... | collective-permute-start | bytes 196616 | tf_op jit(solution)/shard_map/ppermute | solution.py:149
  60.6 6.5 %collective-permute-start.6 = (bf16[128,256]{1,0:T(8,128)(2,1)S(1)}, bf16[128,256]{1,0:T(8,128)(2,1)S(1)}, u32[]{:S(2)}, u32[]{:S(2)}) collective-permute-start(bf16[128,256]{1,0:T(8,128)(2,1)S(1)} %get-tuple-element.25), channel_id=1, source_target_pairs={{0,16},{4,20},{8,24},{12,28},{16,0},{20,4},{24,8},{28,12},{1,17},{... | collective-permute-start | bytes 196616 | tf_op jit(solution)/shard_map/ppermute | solution.py:149
  63.2 6.1 %collective-permute-start.7 = (bf16[128,256]{1,0:T(8,128)(2,1)S(1)}, bf16[128,256]{1,0:T(8,128)(2,1)S(1)}, u32[]{:S(2)}, u32[]{:S(2)}) collective-permute-start(bf16[128,256]{1,0:T(8,128)(2,1)S(1)} %get-tuple-element.24), channel_id=1, source_target_pairs={{0,24},{4,28},{8,16},{12,20},{16,8},{20,12},{24,0},{28,4},{1,25},{... | collective-permute-start | bytes 196616 | tf_op jit(solution)/shard_map/ppermute | solution.py:149
  69.3 3.3 %collective-permute-start.8 = (bf16[32,256]{1,0:T(8,128)(2,1)S(1)}, bf16[32,256]{1,0:T(8,128)(2,1)S(1)}, u32[]{:S(2)}, u32[]{:S(2)}) collective-permute-start(bf16[32,256]{1,0:T(8,128)(2,1)S(1)} %get-tuple-element.28), channel_id=1, source_target_pairs={{0,1},{1,0},{2,3},{3,2},{4,5},{5,4},{6,7},{7,6},{8,9},{9,8},{10,11... | collective-permute-start | bytes 49160 | tf_op jit(solution)/shard_map/ppermute | solution.py:149
  69.4 16.7 %collective-permute-start.1 = (bf16[128,2048]{1,0:T(8,128)(2,1)S(1)}, bf16[128,2048]{1,0:T(8,128)(2,1)S(1)}, u32[]{:S(2)}, u32[]{:S(2)}) collective-permute-start(bf16[128,2048]{1,0:T(8,128)(2,1)S(1)} %copy-done.7), channel_id=1, source_target_pairs={{4,0},{8,4},{12,8},{16,12},{20,16},{24,20},{28,24},{5,1},{9,5},{13... | collective-permute-start | bytes 1572872 | tf_op jit(solution)/shard_map/ppermute | solution.py:154
  70.7 3.8 %collective-permute-start.9 = (bf16[32,256]{1,0:T(8,128)(2,1)S(1)}, bf16[32,256]{1,0:T(8,128)(2,1)S(1)}, u32[]{:S(2)}, u32[]{:S(2)}) collective-permute-start(bf16[32,256]{1,0:T(8,128)(2,1)S(1)} %get-tuple-element.27), channel_id=1, source_target_pairs={{0,2},{1,3},{2,0},{3,1},{4,6},{5,7},{6,4},{7,5},{8,10},{9,11},{10,... | collective-permute-start | bytes 49160 | tf_op jit(solution)/shard_map/ppermute | solution.py:149
  72.3 3.2 %collective-permute-start.10 = (bf16[32,256]{1,0:T(8,128)(2,1)S(1)}, bf16[32,256]{1,0:T(8,128)(2,1)S(1)}, u32[]{:S(2)}, u32[]{:S(2)}) collective-permute-start(bf16[32,256]{1,0:T(8,128)(2,1)S(1)} %get-tuple-element.26), channel_id=1, source_target_pairs={{0,3},{1,2},{2,1},{3,0},{4,7},{5,6},{6,5},{7,4},{8,11},{9,10},{10,... | collective-permute-start | bytes 49160 | tf_op jit(solution)/shard_map/ppermute | solution.py:149
  75.5 31.9 %collective-permute-start.11 = (bf16[4,32,256]{2,1,0:T(8,128)(2,1)S(1)}, bf16[4,32,256]{2,1,0:T(8,128)(2,1)S(1)}, u32[]{:S(2)}, u32[]{:S(2)}) collective-permute-start(bf16[4,32,256]{2,1,0:T(8,128)(2,1)S(1)} %bitcast_dynamic-update-slice_fusion.7), channel_id=1, source_target_pairs={{0,4},{4,0},{8,12},{12,8},{16,20},{20,16},{24,28},{28,24},{1,5},{5... | collective-permute-start | bytes 196616 | tf_op jit(solution)/shard_map/ppermute | solution.py:149
  78.3 30.4 %collective-permute-start.12 = (bf16[4,32,256]{2,1,0:T(8,128)(2,1)S(1)}, bf16[4,32,256]{2,1,0:T(8,128)(2,1)S(1)}, u32[]{:S(2)}, u32[]{:S(2)}) collective-permute-start(bf16[4,32,256]{2,1,0:T(8,128)(2,1)S(1)} %bitcast_dynamic-update-slice_fusion.7), channel_id=1, source_target_pairs={{0,8},{4,12},{8,0},{12,4},{16,24},{20,28},{24,16},{28,20},{1,9},{5... | collective-permute-start | bytes 196616 | tf_op jit(solution)/shard_map/ppermute | solution.py:149
  78.3 33.0 %collective-permute-start.14 = (bf16[4,32,256]{2,1,0:T(8,128)(2,1)S(1)}, bf16[4,32,256]{2,1,0:T(8,128)(2,1)S(1)}, u32[]{:S(2)}, u32[]{:S(2)}) collective-permute-start(bf16[4,32,256]{2,1,0:T(8,128)(2,1)S(1)} %bitcast_dynamic-update-slice_fusion.7), channel_id=1, source_target_pairs={{0,16},{4,20},{8,24},{12,28},{16,0},{20,4},{24,8},{28,12},{1,17},{... | collective-permute-start | bytes 196616 | tf_op jit(solution)/shard_map/ppermute | solution.py:149
  79.7 31.8 %collective-permute-start.16 = (bf16[4,32,256]{2,1,0:T(8,128)(2,1)S(1)}, bf16[4,32,256]{2,1,0:T(8,128)(2,1)S(1)}, u32[]{:S(2)}, u32[]{:S(2)}) collective-permute-start(bf16[4,32,256]{2,1,0:T(8,128)(2,1)S(1)} %bitcast_dynamic-update-slice_fusion.7), channel_id=1, source_target_pairs={{0,24},{4,28},{8,16},{12,20},{16,8},{20,12},{24,0},{28,4},{1,25},{... | collective-permute-start | bytes 196616 | tf_op jit(solution)/shard_map/ppermute | solution.py:149
  104.3 14.2 %collective-permute-start.18 = (f32[3,3,2048]{2,1,0:T(4,128)}, f32[3,3,2048]{2,1,0:T(4,128)S(1)}, u32[]{:S(2)}, u32[]{:S(2)}) collective-permute-start(f32[3,3,2048]{2,1,0:T(4,128)} %get-tuple-element.22), channel_id=1, source_target_pairs={{0,4},{4,0},{8,12},{12,8},{16,20},{20,16},{24,28},{28,24},{1,5},{5... | collective-permute-start | bytes 221192 | tf_op jit(solution)/shard_map/ppermute | solution.py:149
  107.4 6.2 %collective-permute-start.3 = (bf16[3,2,2048]{2,1,0:T(2,128)(2,1)}, bf16[3,2,2048]{2,1,0:T(2,128)(2,1)S(1)}, u32[]{:S(2)}, u32[]{:S(2)}) collective-permute-start(bf16[3,2,2048]{2,1,0:T(2,128)(2,1)} %get-tuple-element.20), channel_id=1, source_target_pairs={{4,0},{8,4},{12,8},{16,12},{20,16},{24,20},{28,24},{5,1},{9,5},{13... | collective-permute-start | bytes 73736 | tf_op jit(solution)/shard_map/ppermute | solution.py:154
  108.7 10.0 %collective-permute-start.13 = (bf16[4,32,256]{2,1,0:T(8,128)(2,1)S(1)}, bf16[4,32,256]{2,1,0:T(8,128)(2,1)S(1)}, u32[]{:S(2)}, u32[]{:S(2)}) collective-permute-start(bf16[4,32,256]{2,1,0:T(8,128)(2,1)S(1)} %collective-permute-done.12), channel_id=1, source_target_pairs={{0,4},{4,0},{8,12},{12,8},{16,20},{20,16},{24,28},{28,24},{1,5},{5... | collective-permute-start | bytes 196616 | tf_op jit(solution)/shard_map/ppermute | solution.py:149
  111.4 7.3 %collective-permute-start.15 = (bf16[4,32,256]{2,1,0:T(8,128)(2,1)S(1)}, bf16[4,32,256]{2,1,0:T(8,128)(2,1)S(1)}, u32[]{:S(2)}, u32[]{:S(2)}) collective-permute-start(bf16[4,32,256]{2,1,0:T(8,128)(2,1)S(1)} %collective-permute-done.14), channel_id=1, source_target_pairs={{0,4},{4,0},{8,12},{12,8},{16,20},{20,16},{24,28},{28,24},{1,5},{5... | collective-permute-start | bytes 196616 | tf_op jit(solution)/shard_map/ppermute | solution.py:149
  111.5 12.2 %collective-permute-start.17 = (bf16[4,32,256]{2,1,0:T(8,128)(2,1)S(1)}, bf16[4,32,256]{2,1,0:T(8,128)(2,1)S(1)}, u32[]{:S(2)}, u32[]{:S(2)}) collective-permute-start(bf16[4,32,256]{2,1,0:T(8,128)(2,1)S(1)} %collective-permute-done.16), channel_id=1, source_target_pairs={{0,4},{4,0},{8,12},{12,8},{16,20},{20,16},{24,28},{28,24},{1,5},{5... | collective-permute-start | bytes 196616 | tf_op jit(solution)/shard_map/ppermute | solution.py:149
  118.6 4.7 %collective-permute-start.19 = (f32[3,3,2048]{2,1,0:T(4,128)S(1)}, f32[3,3,2048]{2,1,0:T(4,128)S(1)}, u32[]{:S(2)}, u32[]{:S(2)}) collective-permute-start(f32[3,3,2048]{2,1,0:T(4,128)S(1)} %add.118), channel_id=1, source_target_pairs={{0,8},{4,12},{8,0},{12,4},{16,24},{20,28},{24,16},{28,20},{1,9},{5... | collective-permute-start | bytes 221192 | tf_op jit(solution)/shard_map/ppermute | solution.py:149
  123.3 6.6 %collective-permute-start.20 = (f32[3,3,2048]{2,1,0:T(4,128)S(1)}, f32[3,3,2048]{2,1,0:T(4,128)S(1)}, u32[]{:S(2)}, u32[]{:S(2)}) collective-permute-start(f32[3,3,2048]{2,1,0:T(4,128)S(1)} %add.119), channel_id=1, source_target_pairs={{0,16},{4,20},{8,24},{12,28},{16,0},{20,4},{24,8},{28,12},{1,17},{... | collective-permute-start | bytes 221192 | tf_op jit(solution)/shard_map/ppermute | solution.py:149
  (6 other events, 8.6 us)
